TPU v7x, 128 devices: a whole 4x4x4 slice. The times are simulated.
128 devices in a mesh: ctx: 32 (over x, y_hi, z), head: 4 (over y_lo, core).
Axes of the slice: x: 4, y: 4 (y_hi: 2, y_lo: 2; y = y_hi * 2 + y_lo), z: 4, core: 2. Of those that a mesh axis runs over, the one named last changes fastest.
Arguments:
- queries: bfloat16 [4096, 4096], P('ctx', 'head'), may hold values from -6 to 6
- keys_new: bfloat16 [4096, 1024], P('ctx', 'head'), may hold values from -6 to 6
- values_new: bfloat16 [4096, 1024], P('ctx', 'head'), may hold values from -6 to 6
- cache_keys: bfloat16 [32768, 1024], P('ctx', 'head'), may hold values from -6 to 6
- cache_values: bfloat16 [32768, 1024], P('ctx', 'head'), may hold values from -6 to 6
- block_list: int32 [8, 32, 64], P('head', 'ctx'), may hold values from -1 to 255, as said below
- block_count: int32 [8, 32], P('head', 'ctx'), may hold values from 0 to 64
- out_weight: bfloat16 [4096, 4096], P('head'), may hold values from -0.21875 to 0.21875
Outputs:
- mixed: bfloat16 [4096, 4096], P(('ctx', 'head'))
Inputs may be any that keep to these rules, and one draw needn't show every extreme that they name: `block_list`: row (h, q) holds distinct cache block numbers in increasing order in its first block_count[h, q] entries and -1 after them. For each KV head, the query blocks of one aligned run of 1 query block together list at most 2 blocks of each aligned run of 8 cache blocks and at least one; for every KV head some run lists exactly 2 of every run of cache blocks.
All inputs are finite; a program needn't handle non-finite values.
Results may differ from a plain program's by a relative error of at most 0.015.
Values may be sent and summed in bfloat16 or wider, within the bound.
No kernel may reach another device: no remote copies, remote signals or barrier semaphores. Data moves between devices by JAX's collectives and lax.ppermute only.
A program may use at most 192 MiB of HBM per device.

v0:
```python
import jax
import jax.numpy as jnp
from jax import lax
from jax.sharding import PartitionSpec as P

HD = 128
BLOCK = 128
CAP = 2
CB_DEV = 8


def passed_along(shard, axis, by):
    devices = lax.axis_size(axis)
    pairs = [(i, i + by) for i in range(devices) if 0 <= i + by < devices]
    return lax.ppermute(shard, axis, pairs)


def wanted(block_rows, counts, block_ids):
    in_use = jnp.arange(block_rows.shape[2])[None, None, :] < counts[:, :, None]
    matches = (block_rows[:, :, :, None] == block_ids[None, None, None, :]) & in_use[:, :, :, None]
    return jnp.any(matches, axis=2)


def slot_table(union_mask):
    position = jnp.cumsum(union_mask.astype(jnp.int32), axis=-1) - 1
    return union_mask[:, :, None, :] & (
        position[:, :, None, :] == jnp.arange(CAP)[None, None, :, None]
    )


def shards(
    queries, keys_new, values_new, cache_keys, cache_values, block_list, block_count, out_weight
):
    n_ctx = lax.axis_size("ctx")
    my_index = lax.axis_index("ctx")
    kv_local = keys_new.shape[1] // HD
    group_size = queries.shape[1] // keys_new.shape[1]
    row_count = queries.shape[0]
    qb_dev = row_count // BLOCK
    nblocks = n_ctx * CB_DEV
    slot_count = n_ctx * CAP
    per_query = wanted(block_list, block_count, jnp.arange(nblocks, dtype=jnp.int32))
    union_mask = jnp.any(per_query, axis=1).reshape(kv_local, n_ctx, CB_DEV)
    picker = slot_table(union_mask)
    per_owner = per_query.reshape(kv_local, qb_dev, n_ctx, CB_DEV)
    listed = jnp.any(picker[:, None] & per_owner[:, :, :, None, :], axis=-1).reshape(
        kv_local, qb_dev, slot_count
    )
    same_owner = jnp.arange(n_ctx)[:, None] == jnp.arange(n_ctx)[None, :]
    pick_global = (
        (picker[:, :, :, None, :] & same_owner[None, :, None, :, None])
        .reshape(kv_local, slot_count, nblocks)
        .astype(jnp.bfloat16)
    )
    pieces = (
        lax.all_gather(cache_keys, "ctx", axis=0, tiled=True),
        lax.all_gather(cache_values, "ctx", axis=0, tiled=True),
    )
    piece_blocks = pieces[0].shape[0] // BLOCK
    piece_keys = pieces[0].reshape(piece_blocks, BLOCK, kv_local, HD)
    piece_values = pieces[1].reshape(piece_blocks, BLOCK, kv_local, HD)
    keys_part = jnp.einsum(
        "hsb,bthd->hstd", pick_global, piece_keys, preferred_element_type=jnp.float32
    ).astype(jnp.bfloat16)
    values_part = jnp.einsum(
        "hsb,bthd->hstd", pick_global, piece_values, preferred_element_type=jnp.float32
    ).astype(jnp.bfloat16)
    prev_keys, prev_values = passed_along((keys_new, values_new), "ctx", 1)
    stretch_keys = jnp.concatenate([prev_keys, keys_new], axis=0)
    stretch_values = jnp.concatenate([prev_values, values_new], axis=0)
    row_ids = jnp.arange(row_count)[:, None]
    key_ids = jnp.arange(BLOCK + row_count)[None, :] - BLOCK
    stretch_ok = (
        (key_ids <= row_ids)
        & (key_ids >= (row_ids // BLOCK - 1) * BLOCK)
        & ((my_index > 0) | (key_ids >= 0))
    )
    score_scale = HD ** (-0.5)
    head_outputs = []
    for kv_head in range(kv_local):
        cache_keyhead = keys_part[kv_head].reshape(slot_count * BLOCK, HD)
        cache_valuehead = values_part[kv_head].reshape(slot_count * BLOCK, HD)
        stretch_keyhead = stretch_keys[:, kv_head * HD : (kv_head + 1) * HD]
        stretch_valuehead = stretch_values[:, kv_head * HD : (kv_head + 1) * HD]
        block_ok = listed[kv_head]
        for member in range(group_size):
            column = (kv_head * group_size + member) * HD
            query_head = queries[:, column : column + HD]
            cache_scores = (
                jnp.einsum(
                    "rd,kd->rk", query_head, cache_keyhead, preferred_element_type=jnp.float32
                )
                * score_scale
            )
            cache_scores = jnp.where(
                block_ok[:, None, :, None],
                cache_scores.reshape(qb_dev, BLOCK, slot_count, BLOCK),
                -jnp.inf,
            ).reshape(row_count, slot_count * BLOCK)
            stretch_scores = (
                jnp.einsum(
                    "rd,kd->rk", query_head, stretch_keyhead, preferred_element_type=jnp.float32
                )
                * score_scale
            )
            stretch_scores = jnp.where(stretch_ok, stretch_scores, -jnp.inf)
            row_max = jnp.maximum(jnp.max(cache_scores, axis=1), jnp.max(stretch_scores, axis=1))[
                :, None
            ]
            cache_weights = jnp.exp(cache_scores - row_max)
            stretch_weights = jnp.exp(stretch_scores - row_max)
            weight_sum = jnp.sum(cache_weights, axis=1) + jnp.sum(stretch_weights, axis=1)
            mixture = jnp.dot(
                cache_weights.astype(jnp.bfloat16),
                cache_valuehead,
                preferred_element_type=jnp.float32,
            )
            mixture = mixture + jnp.dot(
                stretch_weights.astype(jnp.bfloat16),
                stretch_valuehead,
                preferred_element_type=jnp.float32,
            )
            head_outputs.append((mixture / weight_sum[:, None]).astype(jnp.bfloat16))
    attention = jnp.concatenate(head_outputs, axis=1)
    mixed = lax.psum_scatter(
        jnp.dot(attention, out_weight, preferred_element_type=jnp.float32).astype(jnp.bfloat16),
        "head",
        scatter_dimension=0,
        tiled=True,
    )
    return mixed


def solution(mesh):
    return jax.shard_map(
        shards,
        mesh=mesh,
        in_specs=(
            P("ctx", "head"),
            P("ctx", "head"),
            P("ctx", "head"),
            P("ctx", "head"),
            P("ctx", "head"),
            P("head", "ctx", None),
            P("head", "ctx"),
            P("head", None),
        ),
        out_specs=P(("ctx", "head"), None),
        check_vma=False,
    )
```

profile of v0, /device:TPU:1, one launch (start us, length us, event | category | flops | bytes accessed | tf_op | source)
XLA Modules:
  0.0 437.3 jit_solution(14608742840540978373)
XLA Ops:
  8.1 4.4 %collective-permute-start = (bf16[128,256]{1,0:T(8,128)(2,1)}, bf16[128,256]{1,0:T(8,128)(2,1)S(1)}, u32[]{:S(2)}, u32[]{:S(2)}) collective-permute-start(bf16[128,256]{1,0:T(8,128)(2,1)} %param.9), channel_id=1, source_target_pairs={{0,4},{4,8},{8,12},{12,16},{16,20},{20,24},{24,28},{28,32},{32,36}... | collective-permute-start | bytes 196616 | tf_op jit(solution)/shard_map/ppermute | solution.py:15
  12.4 3.5 collective-permute-start.1
  18.3 1.3 and.111
  26.1 142.4 %all-gather.3.cloned.1.call-done = bf16[32768,256]{1,0:T(8,128)(2,1)} async-done(((bf16[1024,256]{1,0:T(8,128)(2,1)}), bf16[32768,256]{1,0:T(8,128)(2,1)}) %all-gather.3.cloned.1.call-update) | async-done | bytes 16777232 | tf_op jit(solution)/shard_map/all_gather | solution.py:56
  168.5 24.3 %reshape.304 = bf16[256,128,2,128]{3,2,1,0:T(2,128)(2,1)} reshape(bf16[32768,256]{1,0:T(8,128)(2,1)} %all-gather.3.cloned.1.call-done) | data formatting | bytes 33554432 | tf_op jit(solution)/shard_map/reshape | solution.py:60
  192.8 24.9 %fusion.28 = bf16[2,64,128,128]{3,1,2,0:T(8,128)(2,1)S(1)} fusion(bf16[256,128,2,128]{3,2,1,0:T(2,128)(2,1)} %reshape.304, pred[2,64,256]{2,1,0:T(32,128)(4,1)S(1)} %and.111, pred[64,256]{1,0:T(8,128)(4,1)S(1)} %and.113), kind=kOutput, calls=%fused_computation.45 | convolution fusion | flops 1075871744 | bytes 21020672 | tf_op jit(solution)/shard_map/hsb,bthd->hstd/dot_general | solution.py:62
  217.7 2.3 fusion.177
  220.0 1.4 copy.22
  221.4 5.6 %fusion.180 = (f32[128]{0:T(128)S(1)}, f32[8192,128]{1,0:T(8,128)}) fusion(bf16[8192,128]{1,0:T(8,128)(2,1)S(1)} %bitcast.71, bf16[128,1024]{1,0:T(8,128)(2,1)S(1)} %copy-done.3, pred[8192]{0:T(1024)(128)(4,1)S(1)} %broadcast_bitcast_fusion.1), kind=kOutput, calls=%fused_computation.220 | convolution fusion | flops 271581056 | bytes 6332928 | tf_op jit(solution)/shard_map/rd,kd->rk/dot_general | solution.py:90
  227.0 5.6 %fusion.182 = (f32[128]{0:T(128)S(1)}, f32[8192,128]{1,0:T(8,128)}) fusion(bf16[8192,128]{1,0:T(8,128)(2,1)S(1)} %bitcast.72, bf16[128,1024]{1,0:T(8,128)(2,1)S(1)} %copy-done.3, pred[8192]{0:T(1024)(128)(4,1)S(1)} %broadcast_bitcast_fusion.1), kind=kOutput, calls=%fused_computation.222 | convolution fusion | flops 271581056 | bytes 6332928 | tf_op jit(solution)/shard_map/rd,kd->rk/dot_general | solution.py:90
  232.5 92.0 %all-gather.5.cloned.1.call-done = bf16[32768,256]{1,0:T(8,128)(2,1)} async-done(((bf16[1024,256]{1,0:T(8,128)(2,1)}), bf16[32768,256]{1,0:T(8,128)(2,1)}) %all-gather.5.cloned.1.call-update) | async-done | bytes 16777232 | tf_op jit(solution)/shard_map/all_gather | solution.py:57
  324.6 23.9 %reshape.305 = bf16[256,128,2,128]{3,2,1,0:T(2,128)(2,1)} reshape(bf16[32768,256]{1,0:T(8,128)(2,1)} %all-gather.5.cloned.1.call-done) | data formatting | bytes 33554432 | tf_op jit(solution)/shard_map/reshape | solution.py:61
  348.5 25.0 %fusion.31 = bf16[2,64,128,128]{3,1,2,0:T(8,128)(2,1)S(1)} fusion(bf16[256,128,2,128]{3,2,1,0:T(2,128)(2,1)} %reshape.305, pred[2,64,256]{2,1,0:T(32,128)(4,1)S(1)} %and.111, pred[64,256]{1,0:T(8,128)(4,1)S(1)} %and.113), kind=kOutput, calls=%fused_computation.46 | convolution fusion | flops 1075871744 | bytes 21020672 | tf_op jit(solution)/shard_map/hsb,bthd->hstd/dot_general | solution.py:65
  374.5 1.4 copy.25
  377.8 1.2 fusion.48
  380.0 1.3 fusion.46
  382.4 1.3 fusion.184
  383.7 1.2 fusion.44
  385.9 1.3 fusion.186
  387.2 1.2 fusion.42
  389.5 1.4 copy.27
  390.8 1.3 fusion.188
  392.1 1.5 fusion.190
  393.6 1.4 copy.28
  396.1 1.2 fusion.40
  397.3 1.2 fusion.38
  399.5 1.3 fusion.192
  400.8 1.2 fusion.36
  403.1 1.3 fusion.194
  404.4 1.4 fusion.34
  409.4 2.3 convolution_convert_fusion
  411.7 18.8 %reduce-scatter.2.cloned.1.call-done = bf16[32,4096]{1,0:T(8,128)(2,1)} async-done(((bf16[128,4096]{1,0:T(8,128)(2,1)}), bf16[32,4096]{1,0:T(8,128)(2,1)}) %reduce-scatter.2.cloned.1.call-update) | async-done | bytes 262160 | tf_op jit(solution)/shard_map/reduce_scatter | solution.py:125
  (102 shorter events, 24.3 us)
Async XLA Ops:
  6.5 18.3 %copy-start.3 = (bf16[128,1024]{1,0:T(8,128)(2,1)S(1)}, bf16[128,1024]{1,0:T(8,128)(2,1)}, u32[]{:S(2)}) copy-start(bf16[128,1024]{1,0:T(8,128)(2,1)} %param.8) | copy-start | bytes 786436
  6.5 162.0 %all-gather.3.cloned.1.call-start = ((), (), s32[]{:S(2)}) async-start(), calls=%async_computation.1 | async-start | bytes 17301504 | tf_op jit(solution)/shard_map/all_gather | solution.py:56
  7.3 317.3 %all-gather.5.cloned.1.call-start = ((), (), s32[]{:S(2)}) async-start(), calls=%async_computation.2 | async-start | bytes 17301504 | tf_op jit(solution)/shard_map/all_gather | solution.py:57
  8.0 422.5 %reduce-scatter.2.cloned.1.call-start = ((), (), s32[]{:S(2)}) async-start(), calls=%async_computation.3 | async-start | bytes 1310720 | tf_op jit(solution)/shard_map/reduce_scatter | solution.py:125
  8.1 13.1 %collective-permute-start = (bf16[128,256]{1,0:T(8,128)(2,1)}, bf16[128,256]{1,0:T(8,128)(2,1)S(1)}, u32[]{:S(2)}, u32[]{:S(2)}) collective-permute-start(bf16[128,256]{1,0:T(8,128)(2,1)} %param.9), channel_id=1, source_target_pairs={{0,4},{4,8},{8,12},{12,16},{16,20},{20,24},{24,28},{28,32},{32,36}... | collective-permute-start | bytes 196616 | tf_op jit(solution)/shard_map/ppermute | solution.py:15
  12.4 9.6 %collective-permute-start.1 = (bf16[128,256]{1,0:T(8,128)(2,1)}, bf16[128,256]{1,0:T(8,128)(2,1)S(1)}, u32[]{:S(2)}, u32[]{:S(2)}) collective-permute-start(bf16[128,256]{1,0:T(8,128)(2,1)} %param.10), channel_id=1, source_target_pairs={{0,4},{4,8},{8,12},{12,16},{16,20},{20,24},{24,28},{28,32},{32,36}... | collective-permute-start | bytes 196616 | tf_op jit(solution)/shard_map/ppermute | solution.py:15
  22.9 169.9 %copy-start.4 = (bf16[256,256]{1,0:T(8,128)(2,1)}, bf16[256,256]{1,0:T(8,128)(2,1)S(1)}, u32[]{:S(2)}) copy-start(bf16[256,256]{1,0:T(8,128)(2,1)S(1)} %constant_dynamic-update-slice_fusion.2) | copy-start | bytes 393220
  374.5 2.2 copy-start.1
  377.8 2.2 copy-start
  387.2 2.3 copy-start.2
  403.1 6.3 %slice-start = ((s8[8388608]{0:T(1024)(128)(4,1)}), s8[4194304]{0:T(1024)(128)(4,1)S(1)}, s32[]{:S(2)}) async-start(s8[8388608]{0:T(1024)(128)(4,1)} %bitcast.87), calls=%async_computation.4 | async-start | bytes 8388608
  404.4 5.0 %slice-start.1 = ((s8[8388608]{0:T(1024)(128)(4,1)}), s8[4194304]{0:T(1024)(128)(4,1)S(1)}, s32[]{:S(2)}) async-start(s8[8388608]{0:T(1024)(128)(4,1)} %bitcast.87), calls=%async_computation.5 | async-start | bytes 8388608
  405.8 1.7 copy-start.5
Sparse Core Ops, SparseCore 0:
  10.5 157.9 all-gather.2
  171.7 152.8 all-gather.4
  411.9 18.6 reduce-scatter.1
where the time goes:
time: 443 us; the launch traced here: 437 us
  waiting for transfers between devices  255 us (58%)
  matrix products  86 us (19%)
  local copies, waits for them, and re-layouts  63.5 us (14%)
  between operations  13.8 us (3%)
  other arithmetic  11.3 us (3%)
  starting transfers between devices  8 us (2%)
    all_gather x1, waiting for transfers between devices, shards(): lax.all_gather(cache_keys, 'ctx', axis=0, tiled=True)  142 us
    all_gather x1, waiting for transfers between devices, shards(): lax.all_gather(cache_values, 'ctx', axis=0, tiled=True)  92 us
    dot_general x1, matrix products, shards(): jnp.einsum('hsb,bthd->hstd', pick_global, piece_values, preferred_element...  25 us
    dot_general x1, matrix products, shards(): jnp.einsum('hsb,bthd->hstd', pick_global, piece_keys, preferred_element_t...  24.9 us
    reshape x1, local copies, waits for them, and re-layouts, shards(): piece_keys = pieces[0].reshape(piece_blocks, BLOCK, kv_local, HD)  24.3 us
    reshape x1, local copies, waits for them, and re-layouts, shards(): piece_values = pieces[1].reshape(piece_blocks, BLOCK, kv_local, HD)  23.9 us
    dot_general x8, matrix products, shards(): jnp.einsum('rd,kd->rk', query_head, cache_keyhead, preferred_element_type...  19 us
    reduce_scatter x1, waiting for transfers between devices, shards(): lax.psum_scatter(jnp.dot(attention, out_weight, preferred_element_type=jn...  18.8 us
  transfers between devices with their start and end apart: 5, of which 3 were waited for; matrix products, arithmetic and copies ran while one was open for 17% of the time, Pallas kernels for 0%

commit v1 on v0

--- a/solution.py
+++ b/solution.py
@@ -54,7 +54,15 @@
     )
     pieces = (
         lax.all_gather(cache_keys, "ctx", axis=0, tiled=True),
-        lax.all_gather(cache_values, "ctx", axis=0, tiled=True),
+        jnp.concatenate(
+            lax.all_to_all(
+                jnp.stack([cache_values] * lax.axis_size("ctx")),
+                axis_name="ctx",
+                split_axis=0,
+                concat_axis=0,
+            ),
+            axis=0,
+        ),
     )
     piece_blocks = pieces[0].shape[0] // BLOCK
     piece_keys = pieces[0].reshape(piece_blocks, BLOCK, kv_local, HD)

time: 443 us -> 606 us (1.37)
  waiting for transfers between devices: 255 us -> 384 us
  local copies, waits for them, and re-layouts: 63.5 us -> 113 us
  matrix products: 86 us -> 59 us
  starting transfers between devices: 8 us -> 17.8 us
    all_to_all x0 -> x1, waiting for transfers between devices: none -> 184 us  [shards(): lax.all_to_all(jnp.stack([cache_values] * lax.axis_size('ctx')), axis_nam...]
    ppermute x2, waiting for transfers between devices: 0.01 us -> 143 us  [passed_along(): return lax.ppermute(shard, axis, pairs)]
    all_gather x1, waiting for transfers between devices: 142 us -> 0.02 us  [shards(): lax.all_gather(cache_keys, 'ctx', axis=0, tiled=True)]
    all_gather x1 -> x0, waiting for transfers between devices: 92 us -> none  [shards(): lax.all_gather(cache_values, 'ctx', axis=0, tiled=True)]
    another operation x0 -> x3, local copies, waits for them, and re-layouts: none -> 56 us  [the longest x2 50 us: shards(): piece_values = pieces[1].reshape(piece_blocks, BLOCK, kv_local, HD)]
    reduce_scatter x1, waiting for transfers between devices: 18.8 us -> 56.5 us  [shards(): lax.psum_scatter(jnp.dot(attention, out_weight, preferred_element_type=jn...]
    reshape x1 -> x0, local copies, waits for them, and re-layouts: 23.9 us -> none  [shards(): piece_values = pieces[1].reshape(piece_blocks, BLOCK, kv_local, HD)]
    all_to_all x0 -> x1, local copies, waits for them, and re-layouts: none -> 18.8 us  [shards(): lax.all_to_all(jnp.stack([cache_values] * lax.axis_size('ctx')), axis_nam...]
  transfers between devices with their start and end apart: 5 -> 5, of which waited for: 3 -> 4; matrix products, arithmetic and copies ran while one was open for 17% -> 16% of each run, Pallas kernels for 0% -> 0%
where the time goes in v1:
time: 606 us; the launch traced here: 598 us
  waiting for transfers between devices  384 us (63%)
  local copies, waits for them, and re-layouts  113 us (19%)
  matrix products  59 us (10%)
  starting transfers between devices  17.8 us (3%)
  between operations  14.1 us (2%)
  other arithmetic  10.2 us (2%)
    all_to_all x1, waiting for transfers between devices, shards(): lax.all_to_all(jnp.stack([cache_values] * lax.axis_size('ctx')), axis_nam...  184 us
    ppermute x2, waiting for transfers between devices, passed_along(): return lax.ppermute(shard, axis, pairs)  143 us
    reduce_scatter x1, waiting for transfers between devices, shards(): lax.psum_scatter(jnp.dot(attention, out_weight, preferred_element_type=jn...  56.5 us
    another operation x2, local copies, waits for them, and re-layouts, shards(): piece_values = pieces[1].reshape(piece_blocks, BLOCK, kv_local, HD)  50 us
    dot_general x1, matrix products, shards(): jnp.einsum('hsb,bthd->hstd', pick_global, piece_keys, preferred_element_t...  24.8 us
    reshape x1, local copies, waits for them, and re-layouts, shards(): piece_keys = pieces[0].reshape(piece_blocks, BLOCK, kv_local, HD)  24.2 us
    all_to_all x1, local copies, waits for them, and re-layouts, shards(): lax.all_to_all(jnp.stack([cache_values] * lax.axis_size('ctx')), axis_nam...  18.8 us
  transfers between devices with their start and end apart: 5, of which 4 were waited for; matrix products, arithmetic and copies ran while one was open for 16% of the time, Pallas kernels for 0%

profile of v1, /device:TPU:1, one launch (start us, length us, event | category | flops | bytes accessed | tf_op | source)
XLA Modules:
  0.0 598.0 jit_solution(924320827280614133)
XLA Ops:
  7.3 1.2 copy.32
  8.5 6.0 stack.2
  14.5 11.6 %all-to-all-start = ((bf16[32,1024,256]{1,2,0:T(8,128)(2,1)}), bf16[32,1024,256]{1,2,0:T(8,128)(2,1)}, u32[]{:S(2)}, u32[]{:S(2)}) async-start(bf16[32,1024,256]{1,2,0:T(8,128)(2,1)} %stack.2), calls=%async_computation | async-start | bytes 33554432 | tf_op jit(solution)/shard_map/all_to_all | solution.py:58
  26.2 3.1 collective-permute-start
  29.3 3.1 collective-permute-start.1
  33.4 1.3 and.111
  36.2 141.5 %collective-permute-done = bf16[128,256]{1,0:T(8,128)(2,1)S(1)} collective-permute-done((bf16[128,256]{1,0:T(8,128)(2,1)S(1)}, bf16[128,256]{1,0:T(8,128)(2,1)S(1)}, u32[]{:S(2)}, u32[]{:S(2)}) %collective-permute-start) | collective-permute-done | bytes 65568 | tf_op jit(solution)/shard_map/ppermute | solution.py:15
  177.8 1.5 collective-permute-done.1
  181.0 183.9 %all-to-all-done = bf16[32,1024,256]{1,2,0:T(8,128)(2,1)} async-done(((bf16[32,1024,256]{1,2,0:T(8,128)(2,1)}), bf16[32,1024,256]{1,2,0:T(8,128)(2,1)}, u32[]{:S(2)}, u32[]{:S(2)}) %all-to-all-start) | async-done | bytes 16777248 | tf_op jit(solution)/shard_map/all_to_all | solution.py:58
  364.9 18.8 %copy.33 = bf16[32,1024,256]{1,0,2:T(8,128)(2,1)} copy(bf16[32,1024,256]{1,2,0:T(8,128)(2,1)} %all-to-all-done) | data formatting | bytes 33554432 | tf_op jit(solution)/shard_map/all_to_all | solution.py:58
  383.7 25.5 %reshape_reshape.3 = bf16[256,128,2,128]{1,0,3,2:T(8,128)(2,1)} reshape(bf16[32,1024,256]{1,0,2:T(8,128)(2,1)} %copy.33) | data formatting | bytes 33554432 | tf_op jit(solution)/shard_map/reshape;reshape | solution.py:69
  409.2 24.5 %copy.34 = bf16[256,128,2,128]{3,0,1,2:T(8,128)(2,1)} copy(bf16[256,128,2,128]{1,0,3,2:T(8,128)(2,1)} %reshape_reshape.3) | data formatting | bytes 33554432 | tf_op jit(solution)/shard_map/reshape;reshape | solution.py:69
  433.8 8.8 %convolution_convert_fusion.1 = bf16[2,64,128,128]{3,1,2,0:T(8,128)(2,1)S(1)} fusion(bf16[256,128,2,128]{3,0,1,2:T(8,128)(2,1)} %copy.34, pred[2,64,256]{2,1,0:T(32,128)(4,1)S(1)} %and.111, pred[64,256]{1,0:T(8,128)(4,1)S(1)} %and.113), kind=kOutput, calls=%fused_computation.44 | convolution fusion | flops 1075871744 | bytes 21020672 | tf_op jit(solution)/shard_map/hsb,bthd->hstd/dot_general | solution.py:73
  443.5 2.7 copy.35
  446.2 1.4 copy.38
  447.5 24.2 %reshape.302 = bf16[256,128,2,128]{3,2,1,0:T(2,128)(2,1)} reshape(bf16[32768,256]{1,0:T(8,128)(2,1)} %all-gather.2.cloned.1.call-done) | data formatting | bytes 33554432 | tf_op jit(solution)/shard_map/reshape | solution.py:68
  471.7 24.8 %fusion.26 = bf16[2,64,128,128]{3,1,2,0:T(8,128)(2,1)S(1)} fusion(bf16[256,128,2,128]{3,2,1,0:T(2,128)(2,1)} %reshape.302, pred[2,64,256]{2,1,0:T(32,128)(4,1)S(1)} %and.111, pred[64,256]{1,0:T(8,128)(4,1)S(1)} %and.113), kind=kOutput, calls=%fused_computation.43 | convolution fusion | flops 1075871744 | bytes 21020672 | tf_op jit(solution)/shard_map/hsb,bthd->hstd/dot_general | solution.py:70
  497.5 1.4 copy.31
  498.9 1.3 fusion.175
  500.1 1.3 fusion.177
  501.4 1.3 fusion.10
  506.4 1.3 fusion.179
  510.0 1.3 fusion.181
  513.5 1.8 copy.37
  515.3 1.3 fusion.183
  516.5 1.3 fusion.185
  518.9 1.2 fusion.35
  522.4 1.3 fusion.187
  525.9 1.3 fusion.189
  527.2 1.3 fusion.29
  532.2 2.3 convolution_convert_fusion
  534.5 56.5 %reduce-scatter.2.cloned.1.call-done = bf16[32,4096]{1,0:T(8,128)(2,1)} async-done(((bf16[128,4096]{1,0:T(8,128)(2,1)}), bf16[32,4096]{1,0:T(8,128)(2,1)}) %reduce-scatter.2.cloned.1.call-update) | async-done | bytes 262160 | tf_op jit(solution)/shard_map/reduce_scatter | solution.py:133
  (109 shorter events, 24.3 us)
Async XLA Ops:
  6.5 441.0 %all-gather.2.cloned.1.call-start = ((), (), s32[]{:S(2)}) async-start(), calls=%async_computation.2 | async-start | bytes 17301504 | tf_op jit(solution)/shard_map/all_gather | solution.py:56
  14.5 11.7 %copy-start.2 = (bf16[128,256]{1,0:T(8,128)(2,1)S(1)}, bf16[128,256]{1,0:T(8,128)(2,1)}, u32[]{:S(2)}) copy-start(bf16[128,256]{1,0:T(8,128)(2,1)} %param.9) | copy-start | bytes 196612
  14.5 14.8 %copy-start.3 = (bf16[128,256]{1,0:T(8,128)(2,1)S(1)}, bf16[128,256]{1,0:T(8,128)(2,1)}, u32[]{:S(2)}) copy-start(bf16[128,256]{1,0:T(8,128)(2,1)} %param.10) | copy-start | bytes 196612
  14.5 17.9 %copy-start.7 = (s32[2,1]{0,1:T(1,128)S(1)}, s32[2,1]{0,1:T(1,128)}, u32[]{:S(2)}) copy-start(s32[2,1]{0,1:T(1,128)} %param.14) | copy-start | bytes 28
  14.5 18.0 %copy-start.6 = (s32[2,1,64]{2,1,0:T(1,128)S(1)}, s32[2,1,64]{2,1,0:T(1,128)}, u32[]{:S(2)}) copy-start(s32[2,1,64]{2,1,0:T(1,128)} %param.13) | copy-start | bytes 1540
  14.5 164.8 %copy-start.1 = (bf16[128,1024]{1,0:T(8,128)(2,1)S(1)}, bf16[128,1024]{1,0:T(8,128)(2,1)}, u32[]{:S(2)}) copy-start(bf16[128,1024]{1,0:T(8,128)(2,1)} %param.8) | copy-start | bytes 786436
  14.5 350.4 %all-to-all-start = ((bf16[32,1024,256]{1,2,0:T(8,128)(2,1)}), bf16[32,1024,256]{1,2,0:T(8,128)(2,1)}, u32[]{:S(2)}, u32[]{:S(2)}) async-start(bf16[32,1024,256]{1,2,0:T(8,128)(2,1)} %stack.2), calls=%async_computation | async-start | bytes 33554432 | tf_op jit(solution)/shard_map/all_to_all | solution.py:58
  26.1 564.9 %reduce-scatter.2.cloned.1.call-start = ((), (), s32[]{:S(2)}) async-start(), calls=%async_computation.3 | async-start | bytes 1310720 | tf_op jit(solution)/shard_map/reduce_scatter | solution.py:133
  26.2 151.6 %collective-permute-start = (bf16[128,256]{1,0:T(8,128)(2,1)S(1)}, bf16[128,256]{1,0:T(8,128)(2,1)S(1)}, u32[]{:S(2)}, u32[]{:S(2)}) collective-permute-start(bf16[128,256]{1,0:T(8,128)(2,1)S(1)} %copy-done.2), channel_id=1, source_target_pairs={{0,4},{4,8},{8,12},{12,16},{16,20},{20,24},{24,28},{28,32},{32,36}... | collective-permute-start | bytes 196616 | tf_op jit(solution)/shard_map/ppermute | solution.py:15
  29.3 150.0 %collective-permute-start.1 = (bf16[128,256]{1,0:T(8,128)(2,1)S(1)}, bf16[128,256]{1,0:T(8,128)(2,1)S(1)}, u32[]{:S(2)}, u32[]{:S(2)}) collective-permute-start(bf16[128,256]{1,0:T(8,128)(2,1)S(1)} %copy-done.3), channel_id=1, source_target_pairs={{0,4},{4,8},{8,12},{12,16},{16,20},{20,24},{24,28},{28,32},{32,36}... | collective-permute-start | bytes 196616 | tf_op jit(solution)/shard_map/ppermute | solution.py:15
  179.3 204.4 %copy-start.4 = (bf16[256,256]{1,0:T(8,128)(2,1)}, bf16[256,256]{1,0:T(8,128)(2,1)S(1)}, u32[]{:S(2)}) copy-start(bf16[256,256]{1,0:T(8,128)(2,1)S(1)} %constant_dynamic-update-slice_fusion.2) | copy-start | bytes 393220
  501.4 1.6 copy-start
  525.9 6.3 %slice-start = ((s8[8388608]{0:T(1024)(128)(4,1)}), s8[4194304]{0:T(1024)(128)(4,1)S(1)}, s32[]{:S(2)}) async-start(s8[8388608]{0:T(1024)(128)(4,1)} %bitcast.90), calls=%async_computation.4 | async-start | bytes 8388608
  527.2 5.0 slice-start.1
  528.6 1.7 copy-start.5
Sparse Core Ops, SparseCore 0:
  10.6 402.0 all-gather.1
  534.6 56.3 reduce-scatter.1
